TPU v7x, 32 devices: a whole 2x2x4 slice. The times are simulated.
32 devices in a mesh: fsdp: 2 (over core), ctx: 4 (over y, x), tp: 4 (over z).
Axes of the slice: x: 2, y: 2, z: 4, core: 2. Of those that a mesh axis runs over, the one named last changes fastest.
Arguments:
- layer_input: float32 [4, 1024, 512], P('fsdp', 'ctx'), may hold values from -6 to 6
- timesteps: int32 [4], P('fsdp'), may hold values from 0 to 999
- segment_ids: int32 [4, 1024], P('fsdp'), may hold values from 0 to 15, never falling along the last dimension, each value on 1 to 512 neighbouring positions
- time_table: float32 [1000, 512], replicated, may hold values from -3 to 3
- ln1_gain: float32 [512], replicated, may hold values from 0.5 to 1.5
- ln1_bias: float32 [512], replicated, may hold values from -1.5 to 1.5
- w_qkv: float32 [3, 512, 512], P(None, 'fsdp', 'tp'), may hold values from -0.25 to 0.25
- b_qv: float32 [2, 512], P(None, 'tp'), may hold values from -1.5 to 1.5
- w_out_t: float32 [512, 512], P('fsdp', 'tp'), may hold values from -1 to 1
- b_out: float32 [512], replicated, may hold values from -1.5 to 1.5
- ln2_gain: float32 [512], replicated, may hold values from 0.5 to 1.5
- ln2_bias: float32 [512], replicated, may hold values from -1.5 to 1.5
- w_up: float32 [512, 2048], P('fsdp', 'tp'), may hold values from -0.25 to 0.25
- b_up: float32 [2048], P('tp'), may hold values from -1.5 to 1.5
- w_down_t: float32 [512, 2048], P('fsdp', 'tp'), may hold values from -0.125 to 0.125
- b_down: float32 [512], replicated, may hold values from -1.5 to 1.5
- out_grad: float32 [4, 1024, 512], P('fsdp', 'ctx'), may hold values from -6 to 6
Outputs:
- output: float32 [4, 1024, 512], P('fsdp', 'ctx')
- grad_input: float32 [4, 1024, 512], P('fsdp', 'ctx')
- grad_table: float32 [1000, 512], replicated
- grad_ln1_gain: float32 [512], replicated
- grad_ln1_bias: float32 [512], replicated
- grad_w_qkv: float32 [3, 512, 512], P(None, 'fsdp', 'tp')
- grad_b_qv: float32 [2, 512], P(None, 'tp')
- grad_w_out_t: float32 [512, 512], P('fsdp', 'tp')
- grad_b_out: float32 [512], replicated
- grad_ln2_gain: float32 [512], replicated
- grad_ln2_bias: float32 [512], replicated
- grad_w_up: float32 [512, 2048], P('fsdp', 'tp')
- grad_b_up: float32 [2048], P('tp')
- grad_w_down_t: float32 [512, 2048], P('fsdp', 'tp')
- grad_b_down: float32 [512], replicated
Inputs may be any that keep to these rules, and one draw needn't show every extreme that they name: `segment_ids`: in each sequence the ids never fall; each document has 1 to 512 characters and one has exactly 512.
All inputs are finite; a program needn't handle non-finite values.
Results may differ from a plain program's by a relative error of at most 0.011.
Values may be sent and summed in bfloat16 or wider, within the bound.
No kernel may reach another device: no remote copies, remote signals or barrier semaphores. Data moves between devices by JAX's collectives and lax.ppermute only.
A program may use at most 64 MiB of HBM per device.

v0:
```python
import jax
import jax.numpy as jnp
from jax import lax
from jax.sharding import PartitionSpec as P

HEAD_DIM = 64
EPSILON = 1e-05
NEGATIVE = -1e30
PRECISE = lax.Precision.HIGHEST


def layer_norm(values, norm_gain, norm_bias):
    centre = values - jnp.mean(values, axis=-1, keepdims=True)
    spread = jnp.mean(centre * centre, axis=-1, keepdims=True)
    return centre * lax.rsqrt(spread + EPSILON) * norm_gain + norm_bias


def contract_last(left, right):
    return lax.dot_general(
        left, right, (((1,), (1,)), ((), ())), preferred_element_type=jnp.float32
    )


def contract_first(left, right):
    return lax.dot_general(
        left, right, (((0,), (0,)), ((), ())), preferred_element_type=jnp.float32
    )


def per_device(
    layer_input,
    timesteps,
    segment_ids,
    time_table,
    ln1_gain,
    ln1_bias,
    w_qkv,
    b_qv,
    w_out_t,
    b_out,
    ln2_gain,
    ln2_bias,
    w_up,
    b_up,
    w_down_t,
    b_down,
    out_grad,
):
    seq_count, span_len, model_width = layer_input.shape
    tok_rows = seq_count * span_len
    seq_len = segment_ids.shape[1]
    step_count = time_table.shape[0]
    ctx_index = lax.axis_index("ctx")
    masters = (
        w_qkv.astype(jnp.bfloat16),
        w_out_t.astype(jnp.bfloat16),
        w_up.astype(jnp.bfloat16),
        w_down_t.astype(jnp.bfloat16),
    )
    qkv_mat, out_mat, up_mat, down_mat = (
        lax.all_gather(masters[0], "fsdp", axis=1, tiled=True),
        lax.all_gather(masters[1], "fsdp", axis=0, tiled=True),
        lax.all_gather(masters[2], "fsdp", axis=0, tiled=True),
        lax.all_gather(masters[3], "fsdp", axis=0, tiled=True),
    )
    steps_hot = (timesteps[:, None] == jnp.arange(step_count, dtype=jnp.int32)[None, :]).astype(
        jnp.float32
    )
    embedded = jnp.dot(steps_hot, time_table, precision=PRECISE)
    stream = (layer_input + embedded[:, None, :]).reshape(tok_rows, model_width)
    normed, norm_one_pull = jax.vjp(layer_norm, stream, ln1_gain, ln1_bias)
    normed_low = normed.astype(jnp.bfloat16)
    projected = jnp.einsum("rd,kdc->krc", normed_low, qkv_mat, preferred_element_type=jnp.float32)
    local_cols = projected.shape[2]
    heads_here = local_cols // HEAD_DIM
    query = (projected[0] + b_qv[0]).astype(jnp.bfloat16)
    key_local = projected[1].astype(jnp.bfloat16).reshape(seq_count, span_len, local_cols)
    value_local = (
        (projected[2] + b_qv[1]).astype(jnp.bfloat16).reshape(seq_count, span_len, local_cols)
    )
    key_all, value_all = (
        lax.all_gather(key_local, "ctx", axis=1, tiled=True),
        lax.all_gather(value_local, "ctx", axis=1, tiled=True),
    )
    query_ids = lax.dynamic_slice_in_dim(segment_ids, ctx_index * span_len, span_len, 1)
    same_doc = (query_ids[:, :, None] == segment_ids[:, None, :])[:, None]
    query_heads = query.reshape(seq_count, span_len, heads_here, HEAD_DIM)
    key_heads = key_all.reshape(seq_count, seq_len, heads_here, HEAD_DIM)
    value_heads = value_all.reshape(seq_count, seq_len, heads_here, HEAD_DIM)
    scale = HEAD_DIM ** (-0.5)

    def score_block():
        raw_scores = jnp.einsum(
            "sqhd,skhd->shqk", query_heads, key_heads, preferred_element_type=jnp.float32
        )
        return jnp.where(same_doc, raw_scores * scale, NEGATIVE)

    scores = score_block()
    row_top = jnp.max(scores, axis=-1, keepdims=True)
    expd = jnp.exp(scores - row_top)
    row_total = jnp.sum(expd, axis=-1, keepdims=True)
    probs = expd / row_total
    log_total = row_top + jnp.log(row_total)
    mixed = jnp.einsum(
        "shqk,skhd->sqhd",
        probs.astype(jnp.bfloat16),
        value_heads,
        preferred_element_type=jnp.float32,
    )
    mixed = mixed.reshape(tok_rows, local_cols).astype(jnp.bfloat16)
    attn_terms = contract_last(mixed, out_mat)
    attn = lax.psum(attn_terms, "tp")
    resid = stream + attn + b_out
    normed_two, norm_two_pull = jax.vjp(layer_norm, resid, ln2_gain, ln2_bias)
    normed_two_low = normed_two.astype(jnp.bfloat16)
    pre_act = jnp.dot(normed_two_low, up_mat, preferred_element_type=jnp.float32) + b_up
    activ, gelu_pull = jax.vjp(jax.nn.gelu, pre_act)
    activ_low = activ.astype(jnp.bfloat16)
    ffn_terms = contract_last(activ_low, down_mat)
    ffn = lax.psum(ffn_terms.astype(jnp.bfloat16), "tp").astype(jnp.float32)
    output = (resid + ffn + b_down).reshape(seq_count, span_len, model_width)
    cotan = out_grad.reshape(tok_rows, model_width)
    cotan_low = cotan.astype(jnp.bfloat16)
    grad_down = contract_first(cotan_low, activ_low)
    grad_act = jnp.dot(cotan_low, down_mat, preferred_element_type=jnp.float32)
    (grad_pre,) = gelu_pull(grad_act)
    grad_pre_low = grad_pre.astype(jnp.bfloat16)
    grad_upmat = contract_first(normed_two_low, grad_pre_low)
    back_two = lax.psum(contract_last(grad_pre_low, up_mat), "tp")
    resid_back, grad_gain_two, grad_bias_two = norm_two_pull(back_two)
    grad_resid = cotan + resid_back
    grad_resid_low = grad_resid.astype(jnp.bfloat16)
    grad_outmat = contract_first(grad_resid_low, mixed)
    grad_mixed = jnp.dot(grad_resid_low, out_mat, preferred_element_type=jnp.float32).astype(
        jnp.bfloat16
    )
    probs_again = jnp.exp(score_block() - log_total)
    mixed_heads = grad_mixed.reshape(seq_count, span_len, heads_here, HEAD_DIM)
    grad_probs = jnp.einsum(
        "sqhd,skhd->shqk", mixed_heads, value_heads, preferred_element_type=jnp.float32
    )
    inner = jnp.sum(probs_again * grad_probs, axis=-1, keepdims=True)
    grad_raw = (probs_again * (grad_probs - inner) * scale).astype(jnp.bfloat16)
    grad_query = jnp.einsum(
        "shqk,skhd->sqhd", grad_raw, key_heads, preferred_element_type=jnp.float32
    ).reshape(tok_rows, local_cols)
    grad_key_all = jnp.einsum(
        "shqk,sqhd->skhd", grad_raw, query_heads, preferred_element_type=jnp.float32
    ).reshape(seq_count, seq_len, local_cols)
    grad_value_all = jnp.einsum(
        "shqk,sqhd->skhd",
        probs_again.astype(jnp.bfloat16),
        mixed_heads,
        preferred_element_type=jnp.float32,
    ).reshape(seq_count, seq_len, local_cols)
    grad_key, grad_value = (
        lax.psum_scatter(grad_key_all, "ctx", scatter_dimension=1, tiled=True),
        lax.psum_scatter(grad_value_all, "ctx", scatter_dimension=1, tiled=True),
    )
    grad_key = grad_key.reshape(tok_rows, local_cols)
    grad_value = grad_value.reshape(tok_rows, local_cols)
    grad_stack = jnp.stack(
        [
            grad_query.astype(jnp.bfloat16),
            grad_key.astype(jnp.bfloat16),
            grad_value.astype(jnp.bfloat16),
        ]
    )
    grad_qkvmat = jnp.einsum(
        "rd,krc->kdc", normed_low, grad_stack, preferred_element_type=jnp.float32
    )
    back_one = lax.psum(
        jnp.einsum("krc,kdc->rd", grad_stack, qkv_mat, preferred_element_type=jnp.float32), "tp"
    )
    stream_back, grad_gain_one, grad_bias_one = norm_one_pull(back_one)
    grad_input = grad_resid + stream_back
    per_sequence = jnp.sum(grad_input.reshape(seq_count, span_len, model_width), axis=1)
    qv_terms = jnp.stack([jnp.sum(grad_query, axis=0), jnp.sum(grad_value, axis=0)])
    small = lax.psum(
        (
            grad_gain_one,
            grad_bias_one,
            grad_gain_two,
            grad_bias_two,
            qv_terms,
            jnp.sum(grad_pre, axis=0),
            jnp.sum(grad_resid, axis=0),
            jnp.sum(cotan, axis=0),
        ),
        ("fsdp", "ctx"),
    )
    (
        gain_one_sum,
        bias_one_sum,
        gain_two_sum,
        bias_two_sum,
        qv_sum,
        up_bias_sum,
        out_bias_sum,
        down_bias_sum,
    ) = small
    table_terms = jnp.dot(steps_hot.T, per_sequence, precision=PRECISE)
    table_sum = lax.psum(table_terms, ("fsdp", "ctx"))
    weight_terms = (grad_qkvmat, grad_outmat, grad_upmat, grad_down)
    summed = lax.psum((weight_terms[0], weight_terms[1], weight_terms[2], weight_terms[3]), "ctx")
    owned = (
        lax.psum_scatter(summed[0], "fsdp", scatter_dimension=1, tiled=True),
        lax.psum_scatter(summed[1], "fsdp", scatter_dimension=0, tiled=True),
        lax.psum_scatter(summed[2], "fsdp", scatter_dimension=0, tiled=True),
        lax.psum_scatter(summed[3], "fsdp", scatter_dimension=0, tiled=True),
    )
    qkv_owned, out_owned, up_owned, down_owned = owned
    return (
        output,
        grad_input.reshape(seq_count, span_len, model_width),
        table_sum,
        gain_one_sum,
        bias_one_sum,
        qkv_owned,
        qv_sum,
        out_owned,
        out_bias_sum,
        gain_two_sum,
        bias_two_sum,
        up_owned,
        up_bias_sum,
        down_owned,
        down_bias_sum,
    )


def solution(mesh):
    placed = (
        P("fsdp", "ctx", None),
        P("fsdp"),
        P("fsdp", None),
        P(),
        P(),
        P(),
        P(None, "fsdp", "tp"),
        P(None, "tp"),
        P("fsdp", "tp"),
        P(),
        P(),
        P(),
        P("fsdp", "tp"),
        P("tp"),
        P("fsdp", "tp"),
        P(),
        P("fsdp", "ctx", None),
    )
    return jax.shard_map(
        per_device,
        mesh=mesh,
        in_specs=placed,
        out_specs=(
            P("fsdp", "ctx", None),
            P("fsdp", "ctx", None),
            P(),
            P(),
            P(),
            P(None, "fsdp", "tp"),
            P(None, "tp"),
            P("fsdp", "tp"),
            P(),
            P(),
            P(),
            P("fsdp", "tp"),
            P("tp"),
            P("fsdp", "tp"),
            P(),
        ),
        check_vma=False,
    )
```

profile of v0, /device:TPU:0, one launch (start us, length us, event | category | flops | bytes accessed | tf_op | source)
XLA Modules:
  0.0 526.8 jit_solution(3402038133135190457)
XLA Ops:
  8.4 2.2 all_gather.18
  21.0 2.1 reshape.228
  25.0 13.5 %all_gather.20 = bf16[2,1024,128]{2,1,0:T(8,128)(2,1)} all-gather(bf16[2,256,128]{2,1,0:T(8,128)(2,1)} %bitcast.102), channel_id=1, replica_groups=mesh['fsdp'=2,'ctx'=4,'tp'=4] {'ctx'}, dimensions={1}, use_global_device_ids=true | all-gather | bytes 655360 | tf_op jit(solution)/shard_map/all_gather | solution.py:82
  41.5 9.8 %all_gather.19 = bf16[2,1024,128]{2,1,0:T(8,128)(2,1)} all-gather(bf16[2,256,128]{2,1,0:T(8,128)(2,1)S(1)} %add_convert_fusion.3), channel_id=1, replica_groups=mesh['fsdp'=2,'ctx'=4,'tp'=4] {'ctx'}, dimensions={1}, use_global_device_ids=true | all-gather | bytes 655360 | tf_op jit(solution)/shard_map/all_gather | solution.py:83
  53.4 2.5 fusion.67
  62.4 2.3 all_gather.22
  64.7 2.3 all_gather.23
  70.8 41.6 %all-reduce.9.cloned.1.call-done = f32[512,512]{1,0:T(8,128)} async-done(((f32[512,512]{1,0:T(8,128)}), f32[512,512]{1,0:T(8,128)}) %all-reduce.9.cloned.1.call-update) | async-done | bytes 1048592 | tf_op jit(solution)/shard_map/psum | solution.py:112
  114.3 2.7 fusion.55
  119.3 2.7 convolution_convert_fusion
  122.3 48.4 %all-reduce.13.cloned.1.call-done = f32[512,512]{1,0:T(8,128)} async-done(((f32[512,512]{1,0:T(8,128)}), f32[512,512]{1,0:T(8,128)}) %all-reduce.13.cloned.1.call-update) | async-done | bytes 1048592 | tf_op jit(solution)/shard_map/psum | solution.py:129
  172.6 38.1 %all-reduce.11.cloned.1.call-done = bf16[512,512]{1,0:T(8,128)(2,1)} async-done(((bf16[512,512]{1,0:T(8,128)(2,1)}), bf16[512,512]{1,0:T(8,128)(2,1)}) %all-reduce.11.cloned.1.call-update) | async-done | bytes 524304 | tf_op jit(solution)/shard_map/psum | solution.py:120
  210.7 3.2 fusion.59
  219.6 4.1 fusion.12
  223.7 3.8 fusion.72
  227.6 12.8 %fusion.7 = f32[2,2,64,1024]{3,2,1,0:T(8,128)} fusion(f32[2,2,256,1024]{3,2,1,0:T(8,128)} %fusion.72, f32[2,2,256,1024]{3,2,1,0:T(8,128)} %copy-done.1, f32[2,2,256]{2,1,0:T(2,128)S(1)} %log_add_fusion, f32[2,256,2,64]{1,3,2,0:T(8,128)} %copy.60, f32[2,64]{1,0:T(2,128)S(1)} %add.179), kind=kOutput, calls=%fused_computation.10 | convolution fusion | flops 141690880 | bytes 9703936 | tf_op jit(solution)/shard_map/shqk,sqhd->skhd/dot_general | solution.py:147
  240.5 2.3 fusion.36
  242.8 2.9 convolution_bitcast_fusion
  245.8 3.1 fusion.39
  248.9 12.1 %fusion.65 = (f32[2,64]{1,0:T(2,128)S(1)}, bf16[2,256,2,64]{1,3,2,0:T(8,128)(2,1)}) fusion(bf16[2,1024,2,64]{1,3,2,0:T(8,128)(2,1)} %bitcast.90, f32[2,2,256,1024]{3,2,1,0:T(8,128)} %fusion.72, f32[2,2,256,1024]{3,2,1,0:T(8,128)} %copy-done.1, f32[2,2,256]{2,1,0:T(2,128)S(1)} %log_add_fusion), kind=kOutput, calls=%fused_computation.104 | convolution fusion | flops 141690752 | bytes 9048576 | tf_op jit(solution)/shard_map/shqk,skhd->sqhd/dot_general | solution.py:144
  268.0 14.4 %reduce-scatter.7.cloned.1.call-done = f32[2,256,128]{1,2,0:T(8,128)} async-done(((f32[2,1024,128]{1,2,0:T(8,128)}), f32[2,256,128]{1,2,0:T(8,128)}) %reduce-scatter.7.cloned.1.call-update) | async-done | bytes 262160 | tf_op jit(solution)/shard_map/reduce_scatter | solution.py:157
  285.6 2.5 convolution_bitcast_fusion.2
  288.2 2.5 convolution_bitcast_fusion.1
  292.7 12.1 %reduce-scatter.17.cloned.1.call-done = f32[256,512]{0,1:T(8,128)} async-done(((f32[512,512]{0,1:T(8,128)}), f32[256,512]{0,1:T(8,128)}) %reduce-scatter.17.cloned.1.call-update) | async-done | bytes 524304 | tf_op jit(solution)/shard_map/reduce_scatter | solution.py:210
  304.8 12.0 %reduce-scatter.15.cloned.1.call-done = f32[256,512]{1,0:T(8,128)} async-done(((f32[512,512]{1,0:T(8,128)}), f32[256,512]{1,0:T(8,128)}) %reduce-scatter.15.cloned.1.call-update) | async-done | bytes 524304 | tf_op jit(solution)/shard_map/reduce_scatter | solution.py:209
  316.7 12.3 %reduce-scatter.11.cloned.1.call-done = f32[3,256,128]{1,2,0:T(8,128)} async-done(((f32[3,512,128]{1,2,0:T(8,128)}), f32[3,256,128]{1,2,0:T(8,128)}) %reduce-scatter.11.cloned.1.call-update) | async-done | bytes 393232 | tf_op jit(solution)/shard_map/reduce_scatter | solution.py:207
  329.4 55.5 %all-reduce.15.cloned.1.call-done = f32[512,512]{1,0:T(8,128)} async-done(((f32[512,512]{1,0:T(8,128)}), f32[512,512]{1,0:T(8,128)}) %all-reduce.15.cloned.1.call-update) | async-done | bytes 1048592 | tf_op jit(solution)/shard_map/psum | solution.py:172
  388.7 2.4 fusion.43
  391.2 27.6 %all-reduce = (f32[512]{0:T(512)}, f32[512]{0:T(512)}, f32[2,128]{1,0:T(2,128)}, f32[512]{0:T(512)}, f32[512]{0:T(512)}, /*index=5*/f32[512]{0:T(512)}, f32[512]{0:T(512)}, f32[512]{0:T(512)}) all-reduce(f32[512]{0:T(512)S(1)} %get-tuple-element.62, ...), channel_id=1, replica_groups=mesh['fsdp'=2,'ctx'=4,'tp'=4] {'fsdp','ctx'}, use_global_device_ids=true, to_apply=%region_20.21 | all-reduce | flops 3840 | bytes 30720 | tf_op jit(solution)/shard_map/psum | solution.py:179
  418.9 31.2 %all-reduce.19.cloned.1.call-done = (f32[3,256,128]{1,2,0:T(8,128)}, f32[256,128]{1,0:T(8,128)}, f32[256,512]{1,0:T(8,128)}, f32[256,512]{0,1:T(8,128)}) async-done(((f32[3,256,128]{1,2,0:T(8,128)}, f32[256,128]{1,0:T(8,128)}, f32[256,512]{1,0:T(8,128)}, f32[256,512]{0,1:T(8,128)}), (f32[3,256,128]{1,2,0:T(8,128)}, f32[256,128]{1,0:T(8,128)}, f32[256,512]{1,0:T(8,128)}, ...) | async-done | bytes 1572880 | tf_op jit(solution)/shard_map/psum | solution.py:205
  454.1 61.3 %all-reduce.17.cloned.1.call-done = f32[1000,512]{1,0:T(8,128)} async-done(((f32[1000,512]{1,0:T(8,128)}), f32[1000,512]{1,0:T(8,128)}) %all-reduce.17.cloned.1.call-update) | async-done | bytes 2048016 | tf_op jit(solution)/shard_map/psum | solution.py:203
  515.4 3.1 copy.92
  (151 shorter events, 63.0 us)
Async XLA Ops:
  7.2 3.4 copy-start
  7.2 6.6 %copy-start.20 = (f32[512]{0:T(512)S(1)}, f32[512]{0:T(512)}, u32[]{:S(2)}) copy-start(f32[512]{0:T(512)} %param.21) | copy-start | bytes 6148
  7.2 6.6 %copy-start.22 = (f32[512]{0:T(512)S(1)}, f32[512]{0:T(512)}, u32[]{:S(2)}) copy-start(f32[512]{0:T(512)} %param.22) | copy-start | bytes 6148
  7.2 105.2 %all-reduce.9.cloned.1.call-start = ((), (), s32[]{:S(2)}) async-start(), calls=%async_computation.6 | async-start | bytes 2097152 | tf_op jit(solution)/shard_map/psum | solution.py:112
  12.0 4.7 copy-start.29
  12.0 7.8 %copy-start.21 = (s32[2,1024]{1,0:T(2,128)S(1)}, s32[2,1024]{1,0:T(2,128)}, u32[]{:S(2)}) copy-start(s32[2,1024]{1,0:T(2,128)} %param.19) | copy-start | bytes 24580
  53.4 3.6 copy-start.8
  60.1 52.3 %copy-start.23 = (f32[512]{0:T(512)S(1)}, f32[512]{0:T(512)}, u32[]{:S(2)}) copy-start(f32[512]{0:T(512)} %param.26) | copy-start | bytes 6148
  60.2 110.5 %all-reduce.13.cloned.1.call-start = ((), (), s32[]{:S(2)}) async-start(), calls=%async_computation.8 | async-start | bytes 2097152 | tf_op jit(solution)/shard_map/psum | solution.py:129
  64.7 49.5 %copy-start.19 = (f32[512]{0:T(512)S(1)}, f32[512]{0:T(512)}, u32[]{:S(2)}) copy-start(f32[512]{0:T(512)} %param.27) | copy-start | bytes 6148
  64.7 49.6 %copy-start.25 = (f32[512]{0:T(512)S(1)}, f32[512]{0:T(512)}, u32[]{:S(2)}) copy-start(f32[512]{0:T(512)} %param.28) | copy-start | bytes 6148
  64.7 49.6 %copy-start.30 = (f32[512]{0:T(512)S(1)}, f32[512]{0:T(512)}, u32[]{:S(2)}) copy-start(f32[512]{0:T(512)} %param.30) | copy-start | bytes 6148
  113.9 3.0 copy-start.2
  117.8 92.9 %copy-start.24 = (f32[512]{0:T(512)S(1)}, f32[512]{0:T(512)}, u32[]{:S(2)}) copy-start(f32[512]{0:T(512)} %param.32) | copy-start | bytes 6148
  119.3 91.4 %all-reduce.11.cloned.1.call-start = ((), (), s32[]{:S(2)}) async-start(), calls=%async_computation.7 | async-start | bytes 1048576 | tf_op jit(solution)/shard_map/psum | solution.py:120
  122.0 142.5 %reduce-scatter.9.cloned.1.call-start = ((), (), s32[]{:S(2)}) async-start(), calls=%async_computation.10 | async-start | bytes 1310720 | tf_op jit(solution)/shard_map/reduce_scatter | solution.py:158
  210.7 3.2 copy-start.6
  210.7 4.5 copy-start.14
  223.7 58.7 %reduce-scatter.7.cloned.1.call-start = ((), (), s32[]{:S(2)}) async-start(), calls=%async_computation.9 | async-start | bytes 1310720 | tf_op jit(solution)/shard_map/reduce_scatter | solution.py:157
  240.4 5.4 %copy-start.26 = (f32[512]{0:T(512)S(1)}, f32[512]{0:T(512)}, u32[]{:S(2)}) copy-start(f32[512]{0:T(512)} %param.28) | copy-start | bytes 6148
  240.4 52.3 %reduce-scatter.13.cloned.1.call-start = ((), (), s32[]{:S(2)}) async-start(), calls=%async_computation.14 | async-start | bytes 393216 | tf_op jit(solution)/shard_map/reduce_scatter | solution.py:208
  242.7 62.0 %reduce-scatter.17.cloned.1.call-start = ((), (), s32[]{:S(2)}) async-start(), calls=%async_computation.16 | async-start | bytes 1572864 | tf_op jit(solution)/shard_map/reduce_scatter | solution.py:210
  245.7 71.0 %reduce-scatter.15.cloned.1.call-start = ((), (), s32[]{:S(2)}) async-start(), calls=%async_computation.15 | async-start | bytes 1572864 | tf_op jit(solution)/shard_map/reduce_scatter | solution.py:209
  248.9 80.2 %reduce-scatter.11.cloned.1.call-start = ((), (), s32[]{:S(2)}) async-start(), calls=%async_computation.13 | async-start | bytes 1179648 | tf_op jit(solution)/shard_map/reduce_scatter | solution.py:207
  288.2 96.7 %all-reduce.15.cloned.1.call-start = ((), (), s32[]{:S(2)}) async-start(), calls=%async_computation.11 | async-start | bytes 2097152 | tf_op jit(solution)/shard_map/psum | solution.py:172
  290.7 159.4 %all-reduce.19.cloned.1.call-start = ((), (), s32[]{:S(2)}) async-start(), calls=%async_computation.17 | async-start | bytes 3145728 | tf_op jit(solution)/shard_map/psum | solution.py:205
  329.1 186.3 %all-reduce.17.cloned.1.call-start = ((), (), s32[]{:S(2)}) async-start(), calls=%async_computation.12 | async-start | bytes 4096000 | tf_op jit(solution)/shard_map/psum | solution.py:203
  384.9 3.6 copy-start.4
  388.4 2.8 copy-start.28
  388.6 129.9 %copy-start.7 = (f32[512,512]{1,0:T(8,128)}, f32[512,512]{1,0:T(8,128)S(1)}, u32[]{:S(2)}) copy-start(f32[512,512]{1,0:T(8,128)S(1)} %add_add_fusion.2) | copy-start | bytes 3145732
  450.1 68.4 %copy-start.18 = (f32[256,128]{1,0:T(8,128)S(1)}, f32[256,128]{1,0:T(8,128)}, u32[]{:S(2)}) copy-start(f32[256,128]{1,0:T(8,128)} %get-tuple-element.117) | copy-start | bytes 393220
  515.4 3.8 copy-start.17
  (11 other events, 15.6 us)
Sparse Core Ops, SparseCore 0:
  60.3 52.0 all-reduce.8
  119.4 51.1 all-reduce.12
  173.0 37.6 all-reduce.10
  223.8 27.7 reduce-scatter.8
  254.6 27.7 reduce-scatter.6
  285.0 7.6 reduce-scatter.12
  295.0 9.6 reduce-scatter.16
  307.0 9.6 reduce-scatter.14
  319.7 9.3 reduce-scatter.10
  331.9 52.9 all-reduce.14
  388.6 61.4 all-reduce.18
  453.8 61.5 all-reduce.16
where the time goes:
time: 528 us; the launch traced here: 527 us
  waiting for transfers between devices  329 us (62%)
  matrix products  64.3 us (12%)
  blocking collectives  59.8 us (11%)
  local copies, waits for them, and re-layouts  33 us (6%)
  other arithmetic  25.2 us (5%)
  between operations  14.6 us (3%)
    psum x1, waiting for transfers between devices, per_device(): table_sum = lax.psum(table_terms, ('fsdp', 'ctx'))  61.3 us
    psum x1, waiting for transfers between devices, per_device(): lax.psum(jnp.einsum('krc,kdc->rd', grad_stack, qkv_mat, preferred_element...  55.5 us
    psum x1, waiting for transfers between devices, per_device(): back_two = lax.psum(contract_last(grad_pre_low, up_mat), 'tp')  48.4 us
    psum x1, waiting for transfers between devices, per_device(): attn = lax.psum(attn_terms, 'tp')  41.6 us
    psum x1, waiting for transfers between devices, per_device(): ffn = lax.psum(ffn_terms.astype(jnp.bfloat16), 'tp').astype(jnp.float32)  38.1 us
    psum x1, waiting for transfers between devices, per_device(): lax.psum((weight_terms[0], weight_terms[1], weight_terms[2], weight_terms...  31.2 us
    psum x1, blocking collectives, per_device(): lax.psum((grad_gain_one, grad_bias_one, grad_gain_two, grad_bias_two, qv_...  27.6 us
    reduce_scatter x1, waiting for transfers between devices, per_device(): lax.psum_scatter(grad_key_all, 'ctx', scatter_dimension=1, tiled=True)  14.4 us
  transfers between devices with their start and end apart: 12, of which 11 were waited for; matrix products, arithmetic and copies ran while one was open for 14% of the time, Pallas kernels for 0%

commit v1 on v0

--- a/solution.py
+++ b/solution.py
@@ -200,7 +200,8 @@
         down_bias_sum,
     ) = small
     table_terms = jnp.dot(steps_hot.T, per_sequence, precision=PRECISE)
-    table_sum = lax.psum(table_terms, ("fsdp", "ctx"))
+    terms = lax.all_gather(table_terms, ("fsdp", "ctx"), axis=0, tiled=False)
+    table_sum = terms.sum(axis=0)
     weight_terms = (grad_qkvmat, grad_outmat, grad_upmat, grad_down)
     summed = lax.psum((weight_terms[0], weight_terms[1], weight_terms[2], weight_terms[3]), "ctx")
     owned = (

time: 528 us -> 547 us (1.036)
  waiting for transfers between devices: 329 us -> 366 us
  local copies, waits for them, and re-layouts: 33 us -> 15.3 us
    all_gather x0 -> x1, waiting for transfers between devices: none -> 86.6 us  [per_device(): terms = lax.all_gather(table_terms, ('fsdp', 'ctx'), axis=0, tiled=False)]
    psum x1 -> x0, waiting for transfers between devices: 61.3 us -> none  [per_device(): table_sum = lax.psum(table_terms, ('fsdp', 'ctx'))]
    reduce_sum x0 -> x1, other arithmetic: none -> 9.38 us  [per_device(): table_sum = terms.sum(axis=0)]
    reduce_scatter x1, waiting for transfers between devices: 14.4 us -> 20.7 us  [per_device(): lax.psum_scatter(grad_key_all, 'ctx', scatter_dimension=1, tiled=True)]
    unnamed x70 -> x65, local copies, waits for them, and re-layouts: 12.7 us -> 9.12 us
  transfers between devices with their start and end apart: 12 -> 12, of which waited for: 11 -> 11; matrix products, arithmetic and copies ran while one was open for 14% -> 11% of each run, Pallas kernels for 0% -> 0%
where the time goes in v1:
time: 547 us; the launch traced here: 545 us
  waiting for transfers between devices  366 us (67%)
  matrix products  59.7 us (11%)
  blocking collectives  58.4 us (11%)
  other arithmetic  30.6 us (6%)
  local copies, waits for them, and re-layouts  15.3 us (3%)
  between operations  14.7 us (3%)
    all_gather x1, waiting for transfers between devices, per_device(): terms = lax.all_gather(table_terms, ('fsdp', 'ctx'), axis=0, tiled=False)  86.6 us
    psum x1, waiting for transfers between devices, per_device(): lax.psum(jnp.einsum('krc,kdc->rd', grad_stack, qkv_mat, preferred_element...  55.5 us
    psum x1, waiting for transfers between devices, per_device(): back_two = lax.psum(contract_last(grad_pre_low, up_mat), 'tp')  48.4 us
    psum x1, waiting for transfers between devices, per_device(): attn = lax.psum(attn_terms, 'tp')  43 us
    psum x1, waiting for transfers between devices, per_device(): ffn = lax.psum(ffn_terms.astype(jnp.bfloat16), 'tp').astype(jnp.float32)  39 us
    psum x1, waiting for transfers between devices, per_device(): lax.psum((weight_terms[0], weight_terms[1], weight_terms[2], weight_terms...  30.3 us
    psum x1, blocking collectives, per_device(): lax.psum((grad_gain_one, grad_bias_one, grad_gain_two, grad_bias_two, qv_...  27.7 us
    reduce_scatter x1, waiting for transfers between devices, per_device(): lax.psum_scatter(grad_key_all, 'ctx', scatter_dimension=1, tiled=True)  20.7 us
  transfers between devices with their start and end apart: 12, of which 11 were waited for; matrix products, arithmetic and copies ran while one was open for 11% of the time, Pallas kernels for 0%

profile of v1, /device:TPU:0, one launch (start us, length us, event | category | flops | bytes accessed | tf_op | source)
XLA Modules:
  0.0 545.5 jit_solution(15708354884964933504)
XLA Ops:
  8.4 2.2 all_gather.24
  16.0 1.9 all_gather.27
  19.6 12.3 %all_gather.26 = bf16[2,1024,128]{2,1,0:T(8,128)(2,1)S(1)} all-gather(bf16[2,256,128]{2,1,0:T(8,128)(2,1)} %bitcast.104), channel_id=1, replica_groups=mesh['fsdp'=2,'ctx'=4,'tp'=4] {'ctx'}, dimensions={1}, use_global_device_ids=true | all-gather | bytes 655360 | tf_op jit(solution)/shard_map/all_gather | solution.py:82
  33.3 9.8 %all_gather.25 = bf16[2,1024,128]{2,1,0:T(8,128)(2,1)} all-gather(bf16[2,256,128]{2,1,0:T(8,128)(2,1)S(1)} %add_convert_fusion.3), channel_id=1, replica_groups=mesh['fsdp'=2,'ctx'=4,'tp'=4] {'ctx'}, dimensions={1}, use_global_device_ids=true | all-gather | bytes 655360 | tf_op jit(solution)/shard_map/all_gather | solution.py:83
  44.4 2.4 fusion.67
  52.6 2.3 all_gather.28
  55.0 2.3 all_gather.29
  59.6 43.0 %all-reduce.8.cloned.1.call-done = f32[512,512]{1,0:T(8,128)} async-done(((f32[512,512]{1,0:T(8,128)}), f32[512,512]{1,0:T(8,128)}) %all-reduce.8.cloned.1.call-update) | async-done | bytes 1048592 | tf_op jit(solution)/shard_map/psum | solution.py:112
  104.5 2.1 fusion.55
  109.0 2.7 convolution_convert_fusion
  112.0 48.4 %all-reduce.12.cloned.1.call-done = f32[512,512]{1,0:T(8,128)} async-done(((f32[512,512]{1,0:T(8,128)}), f32[512,512]{1,0:T(8,128)}) %all-reduce.12.cloned.1.call-update) | async-done | bytes 1048592 | tf_op jit(solution)/shard_map/psum | solution.py:129
  162.0 39.0 %all-reduce.10.cloned.1.call-done = bf16[512,512]{1,0:T(8,128)(2,1)} async-done(((bf16[512,512]{1,0:T(8,128)(2,1)}), bf16[512,512]{1,0:T(8,128)(2,1)}) %all-reduce.10.cloned.1.call-update) | async-done | bytes 524304 | tf_op jit(solution)/shard_map/psum | solution.py:120
  201.0 2.9 fusion.59
  207.2 4.1 fusion.12
  211.4 3.8 fusion.72
  215.2 12.8 %fusion.7 = f32[2,2,64,1024]{3,2,1,0:T(8,128)} fusion(f32[2,2,256,1024]{3,2,1,0:T(8,128)} %fusion.72, f32[2,2,256,1024]{3,2,1,0:T(8,128)} %copy-done.2, f32[2,2,256]{2,1,0:T(2,128)S(1)} %log_add_fusion, f32[2,256,2,64]{1,3,2,0:T(8,128)} %copy-done.14, f32[2,64]{1,0:T(2,128)S(1)} %add.177), kind=kOutput, calls=%fused_computation.10 | convolution fusion | flops 141690880 | bytes 9703936 | tf_op jit(solution)/shard_map/shqk,sqhd->skhd/dot_general | solution.py:147
  228.1 2.3 fusion.36
  230.4 2.9 convolution_bitcast_fusion
  233.4 2.7 fusion.39
  236.1 11.5 %fusion.65 = (f32[2,64]{1,0:T(2,128)S(1)}, bf16[2,256,2,64]{1,3,2,0:T(8,128)(2,1)S(1)}) fusion(bf16[2,1024,2,64]{1,3,2,0:T(8,128)(2,1)} %bitcast.92, f32[2,2,256,1024]{3,2,1,0:T(8,128)} %fusion.72, f32[2,2,256,1024]{3,2,1,0:T(8,128)} %copy-done.2, f32[2,2,256]{2,1,0:T(2,128)S(1)} %log_add_fusion), kind=kOutput, calls=%fused_computation.104 | convolution fusion | flops 141690752 | bytes 9048576 | tf_op jit(solution)/shard_map/shqk,skhd->sqhd/dot_general | solution.py:144
  249.4 20.7 %reduce-scatter.7.cloned.1.call-done = f32[2,256,128]{1,2,0:T(8,128)} async-done(((f32[2,1024,128]{1,2,0:T(8,128)}), f32[2,256,128]{1,2,0:T(8,128)}) %reduce-scatter.7.cloned.1.call-update) | async-done | bytes 262160 | tf_op jit(solution)/shard_map/reduce_scatter | solution.py:157
  274.0 6.4 %reduce-scatter.13.cloned.1.call-done = f32[256,128]{1,0:T(8,128)} async-done(((f32[512,128]{1,0:T(8,128)}), f32[256,128]{1,0:T(8,128)}) %reduce-scatter.13.cloned.1.call-update) | async-done | bytes 131088 | tf_op jit(solution)/shard_map/reduce_scatter | solution.py:209
  280.4 12.1 %reduce-scatter.17.cloned.1.call-done = f32[256,512]{0,1:T(8,128)} async-done(((f32[512,512]{0,1:T(8,128)}), f32[256,512]{0,1:T(8,128)}) %reduce-scatter.17.cloned.1.call-update) | async-done | bytes 524304 | tf_op jit(solution)/shard_map/reduce_scatter | solution.py:211
  292.5 12.0 %reduce-scatter.15.cloned.1.call-done = f32[256,512]{1,0:T(8,128)} async-done(((f32[512,512]{1,0:T(8,128)}), f32[256,512]{1,0:T(8,128)}) %reduce-scatter.15.cloned.1.call-update) | async-done | bytes 524304 | tf_op jit(solution)/shard_map/reduce_scatter | solution.py:210
  304.4 11.8 %reduce-scatter.11.cloned.1.call-done = f32[3,256,128]{1,2,0:T(8,128)} async-done(((f32[3,512,128]{1,2,0:T(8,128)}), f32[3,256,128]{1,2,0:T(8,128)}) %reduce-scatter.11.cloned.1.call-update) | async-done | bytes 393232 | tf_op jit(solution)/shard_map/reduce_scatter | solution.py:208
  316.5 55.5 %all-reduce.14.cloned.1.call-done = f32[512,512]{1,0:T(8,128)} async-done(((f32[512,512]{1,0:T(8,128)}), f32[512,512]{1,0:T(8,128)}) %all-reduce.14.cloned.1.call-update) | async-done | bytes 1048592 | tf_op jit(solution)/shard_map/psum | solution.py:172
  376.8 2.4 fusion.43
  379.3 27.7 %all-reduce = (f32[512]{0:T(512)}, f32[512]{0:T(512)}, f32[2,128]{1,0:T(2,128)}, f32[512]{0:T(512)}, f32[512]{0:T(512)}, /*index=5*/f32[512]{0:T(512)}, f32[512]{0:T(512)}, f32[512]{0:T(512)}) all-reduce(f32[512]{0:T(512)S(1)} %get-tuple-element.62, ...), channel_id=1, replica_groups=mesh['fsdp'=2,'ctx'=4,'tp'=4] {'fsdp','ctx'}, use_global_device_ids=true, to_apply=%region_20.21 | all-reduce | flops 3840 | bytes 30720 | tf_op jit(solution)/shard_map/psum | solution.py:179
  406.9 30.3 %all-reduce.16.cloned.1.call-done = (f32[3,256,128]{1,2,0:T(8,128)}, f32[256,128]{1,0:T(8,128)}, f32[256,512]{1,0:T(8,128)}, f32[256,512]{0,1:T(8,128)}) async-done(((f32[3,256,128]{1,2,0:T(8,128)}, f32[256,128]{1,0:T(8,128)}, f32[256,512]{1,0:T(8,128)}, f32[256,512]{0,1:T(8,128)}), (f32[3,256,128]{1,2,0:T(8,128)}, f32[256,128]{1,0:T(8,128)}, f32[256,512]{1,0:T(8,128)}, ...) | async-done | bytes 1572880 | tf_op jit(solution)/shard_map/psum | solution.py:206
  439.2 2.0 copy.72
  441.2 86.6 %all-gather.3.cloned.1.call-done = f32[8000,512]{1,0:T(8,128)} async-done(((f32[1000,512]{1,0:T(8,128)}), f32[8000,512]{1,0:T(8,128)}) %all-gather.3.cloned.1.call-update) | async-done | bytes 16384016 | tf_op jit(solution)/shard_map/all_gather | solution.py:203
  527.8 9.4 %reduce_sum.232 = f32[1000,512]{1,0:T(8,128)} reduce(f32[8,1000,512]{2,1,0:T(8,128)} %bitcast.88, f32[]{:T(128)} %constant.11.clone.1), dimensions={0}, to_apply=%region_18.19 | reduce | flops 3584000 | bytes 18432004 | tf_op jit(solution)/shard_map/reduce_sum | solution.py:204
  (147 shorter events, 42.9 us)
Async XLA Ops:
  7.2 3.4 copy-start
  7.2 6.6 %copy-start.20 = (f32[512]{0:T(512)S(1)}, f32[512]{0:T(512)}, u32[]{:S(2)}) copy-start(f32[512]{0:T(512)} %param.21) | copy-start | bytes 6148
  7.2 6.6 %copy-start.22 = (f32[512]{0:T(512)S(1)}, f32[512]{0:T(512)}, u32[]{:S(2)}) copy-start(f32[512]{0:T(512)} %param.22) | copy-start | bytes 6148
  7.2 95.5 %all-reduce.8.cloned.1.call-start = ((), (), s32[]{:S(2)}) async-start(), calls=%async_computation.6 | async-start | bytes 2097152 | tf_op jit(solution)/shard_map/psum | solution.py:112
  12.0 3.9 copy-start.27
  12.1 4.0 copy-start.17
  12.1 5.9 %copy-start.21 = (s32[2,1024]{1,0:T(2,128)S(1)}, s32[2,1024]{1,0:T(2,128)}, u32[]{:S(2)}) copy-start(s32[2,1024]{1,0:T(2,128)} %param.19) | copy-start | bytes 24580
  19.6 27.1 %copy-start.14 = (f32[2,256,2,64]{1,3,2,0:T(8,128)}, f32[2,256,2,64]{1,3,2,0:T(8,128)S(1)}, u32[]{:S(2)}) copy-start(f32[2,256,2,64]{1,3,2,0:T(8,128)S(1)} %copy.60) | copy-start | bytes 786436
  32.1 15.7 %copy-start.8 = (bf16[2,1024,128]{1,2,0:T(8,128)(2,1)}, bf16[2,1024,128]{1,2,0:T(8,128)(2,1)S(1)}, u32[]{:S(2)}) copy-start(bf16[2,1024,128]{1,2,0:T(8,128)(2,1)S(1)} %copy.61) | copy-start | bytes 1572868
  44.4 3.5 copy-start.9
  48.9 8.3 %copy-start.5 = (f32[2,256,512]{2,1,0:T(8,128)S(1)}, f32[2,256,512]{2,1,0:T(8,128)}, u32[]{:S(2)}) copy-start(f32[2,256,512]{2,1,0:T(8,128)} %param.33) | copy-start | bytes 3145732
  50.4 52.3 %copy-start.23 = (f32[512]{0:T(512)S(1)}, f32[512]{0:T(512)}, u32[]{:S(2)}) copy-start(f32[512]{0:T(512)} %param.26) | copy-start | bytes 6148
  50.4 109.9 %all-reduce.12.cloned.1.call-start = ((), (), s32[]{:S(2)}) async-start(), calls=%async_computation.8 | async-start | bytes 2097152 | tf_op jit(solution)/shard_map/psum | solution.py:129
  54.9 49.5 %copy-start.19 = (f32[512]{0:T(512)S(1)}, f32[512]{0:T(512)}, u32[]{:S(2)}) copy-start(f32[512]{0:T(512)} %param.27) | copy-start | bytes 6148
  55.0 49.5 %copy-start.25 = (f32[512]{0:T(512)S(1)}, f32[512]{0:T(512)}, u32[]{:S(2)}) copy-start(f32[512]{0:T(512)} %param.28) | copy-start | bytes 6148
  55.0 49.6 %copy-start.28 = (f32[512]{0:T(512)S(1)}, f32[512]{0:T(512)}, u32[]{:S(2)}) copy-start(f32[512]{0:T(512)} %param.30) | copy-start | bytes 6148
  107.5 93.5 %copy-start.24 = (f32[512]{0:T(512)S(1)}, f32[512]{0:T(512)}, u32[]{:S(2)}) copy-start(f32[512]{0:T(512)} %param.32) | copy-start | bytes 6148
  109.0 92.0 %all-reduce.10.cloned.1.call-start = ((), (), s32[]{:S(2)}) async-start(), calls=%async_computation.7 | async-start | bytes 1048576 | tf_op jit(solution)/shard_map/psum | solution.py:120
  111.7 136.3 %reduce-scatter.9.cloned.1.call-start = ((), (), s32[]{:S(2)}) async-start(), calls=%async_computation.10 | async-start | bytes 1310720 | tf_op jit(solution)/shard_map/reduce_scatter | solution.py:158
  211.4 58.7 %reduce-scatter.7.cloned.1.call-start = ((), (), s32[]{:S(2)}) async-start(), calls=%async_computation.9 | async-start | bytes 1310720 | tf_op jit(solution)/shard_map/reduce_scatter | solution.py:157
  228.0 52.4 %reduce-scatter.13.cloned.1.call-start = ((), (), s32[]{:S(2)}) async-start(), calls=%async_computation.14 | async-start | bytes 393216 | tf_op jit(solution)/shard_map/reduce_scatter | solution.py:209
  230.4 62.1 %reduce-scatter.17.cloned.1.call-start = ((), (), s32[]{:S(2)}) async-start(), calls=%async_computation.16 | async-start | bytes 1572864 | tf_op jit(solution)/shard_map/reduce_scatter | solution.py:211
  233.3 71.1 %reduce-scatter.15.cloned.1.call-start = ((), (), s32[]{:S(2)}) async-start(), calls=%async_computation.15 | async-start | bytes 1572864 | tf_op jit(solution)/shard_map/reduce_scatter | solution.py:210
  236.1 80.1 %reduce-scatter.11.cloned.1.call-start = ((), (), s32[]{:S(2)}) async-start(), calls=%async_computation.13 | async-start | bytes 1179648 | tf_op jit(solution)/shard_map/reduce_scatter | solution.py:208
  272.5 99.5 %all-reduce.14.cloned.1.call-start = ((), (), s32[]{:S(2)}) async-start(), calls=%async_computation.11 | async-start | bytes 2097152 | tf_op jit(solution)/shard_map/psum | solution.py:172
  274.0 101.5 %copy-start.4 = (f32[512,512]{1,0:T(8,128)S(1)}, f32[512,512]{1,0:T(8,128)}, u32[]{:S(2)}) copy-start(f32[512,512]{1,0:T(8,128)} %copy-done.3) | copy-start | bytes 3145732
  274.0 163.3 %all-reduce.16.cloned.1.call-start = ((), (), s32[]{:S(2)}) async-start(), calls=%async_computation.17 | async-start | bytes 3145728 | tf_op jit(solution)/shard_map/psum | solution.py:206
  316.3 211.5 %all-gather.3.cloned.1.call-start = ((), (), s32[]{:S(2)}) async-start(), calls=%async_computation.12 | async-start | bytes 18432000 | tf_op jit(solution)/shard_map/all_gather | solution.py:203
  373.7 3.1 copy-start.26
  527.8 9.4 %copy-start.18 = (f32[256,128]{1,0:T(8,128)S(1)}, f32[256,128]{1,0:T(8,128)}, u32[]{:S(2)}) copy-start(f32[256,128]{1,0:T(8,128)} %get-tuple-element.117) | copy-start | bytes 393220
  527.8 10.0 %copy-start.16 = (f32[256,512]{1,0:T(8,128)S(1)}, f32[256,512]{1,0:T(8,128)}, u32[]{:S(2)}) copy-start(f32[256,512]{1,0:T(8,128)} %get-tuple-element.121) | copy-start | bytes 1572868
  527.8 10.8 %copy-start.1 = (f32[1000,512]{1,0:T(8,128)S(1)}, f32[1000,512]{1,0:T(8,128)}, u32[]{:S(2)}) copy-start(f32[1000,512]{1,0:T(8,128)} %param.20) | copy-start | bytes 6144004
  (9 other events, 13.1 us)
Sparse Core Ops, SparseCore 0:
  50.5 52.0 all-reduce.7
  109.1 51.1 all-reduce.11
  163.3 37.6 all-reduce.9
  211.5 27.7 reduce-scatter.8
  242.2 27.7 reduce-scatter.6
  272.7 7.6 reduce-scatter.12
  282.8 9.6 reduce-scatter.16
  294.7 9.6 reduce-scatter.14
  306.8 9.3 reduce-scatter.10
  319.0 52.9 all-reduce.13
  375.7 61.4 all-reduce.15
  439.6 88.1 all-gather.2
